TPU v7x, 32 devices: a whole 2x2x4 slice. The times are simulated.
32 devices in a mesh: scene: 8 (over z, y), image: 4 (over x, core).
Axes of the slice: x: 2, y: 2, z: 4, core: 2. Of those that a mesh axis runs over, the one named last changes fastest.
Arguments:
- jacobian: bfloat16 [256, 256, 1152], P(('scene', 'image')), may hold values from -0.1875 to 0.1875
- splat_ids: int32 [256, 128], P(('scene', 'image')), may hold values from 0 to 8191, as said below
- pix_residual: bfloat16 [256, 256], P(('scene', 'image')), may hold values from -6 to 6
- live_blocks: int32 [32], replicated, may hold values from 1 to 8, as said below
- proj_jac: bfloat16 [9, 59, 8192], P(None, None, 'scene'), may hold values from -0.75 to 0.75
- damping: float32 [59, 8192], P(None, 'scene'), may hold values from 0.1 to 1
- precond: float32 [59, 8192], P(None, 'scene'), may hold values from 0.3 to 9
Outputs:
- solution: float32 [59, 8192], P(None, 'scene')
- residual: float32 [59, 8192], P(None, 'scene')
Inputs may be any that keep to these rules, and one draw needn't show every extreme that they name: live_blocks[d] counts the blocks in use on device d = scene index * 4 + image index; they are its slots 0 to live_blocks[d] - 1; some device uses all 8 while the device whose index differs from it in the lowest bit uses at most half of them. `splat_ids`: splat s of every block names a Gaussian of scene index s // 16, that is an id from that index times 1024 to the next such multiple.
All inputs are finite; a program needn't handle non-finite values.
Results may differ from a plain program's by a relative error of at most 0.0051.
Values may be sent and summed in bfloat16 or wider, within the bound.
A program may use at most 64 MiB of HBM per device.

v0:
```python
import jax
import jax.numpy as jnp
from jax import lax
from jax.sharding import PartitionSpec as P

ITERS = 2


def project(proj_jac, field):
    return jnp.einsum(
        "kag,ag->kg", proj_jac.astype(jnp.float32), field, precision=lax.Precision.HIGHEST
    ).astype(jnp.bfloat16)


def lift(proj_jac, weights):
    return jnp.einsum(
        "kag,kg->ag", proj_jac.astype(jnp.float32), weights, precision=lax.Precision.HIGHEST
    )


def run_blocks(jac_set, pixel_set, first_pos, last_pos, picker, keeper, initial):

    def advance(position, running):
        jac_block = lax.dynamic_index_in_dim(jac_set, position, 0, keepdims=False)
        if picker is None:
            signal = lax.dynamic_index_in_dim(pixel_set, position, 0, keepdims=False)
        else:
            signal = jnp.dot(
                jac_block, picker(position), preferred_element_type=jnp.float32
            ).astype(jnp.bfloat16)
        returned = jnp.dot(signal, jac_block, preferred_element_type=jnp.float32)
        return keeper(running, position, returned)

    return lax.fori_loop(first_pos, last_pos, advance, initial)


def local(jacobian, splat_ids, pix_residual, live_blocks, proj_jac, damping, precond):
    g_dev = damping.shape[1]
    n_proj = proj_jac.shape[0]
    n_scene = lax.axis_size("scene")
    owner_width = splat_ids.shape[1] // n_scene
    scene_pos = lax.axis_index("scene")
    device_pos = scene_pos * lax.axis_size("image") + lax.axis_index("image")
    own_live = live_blocks[device_pos]
    block_sets = [(jacobian, splat_ids, pix_residual, 0, own_live)]
    offsets = []
    total_slots = 0
    member = block_sets[0]
    offsets.append(total_slots)
    total_slots += member[0].shape[0]
    ids_all = jnp.concatenate([member[1] for member in block_sets], axis=0)
    routed_ids = lax.all_to_all(
        ids_all.reshape(total_slots, n_scene, owner_width),
        "scene",
        split_axis=1,
        concat_axis=1,
        tiled=True,
    )
    local_ids = routed_ids - scene_pos * g_dev

    def back_project(source):
        buffer = jnp.zeros((total_slots, n_proj, n_scene, owner_width), jnp.float32)
        for index_set, (jac_set, id_set, pixel_set, first_pos, last_pos) in enumerate(block_sets):
            slot_base = offsets[index_set]

            def keeper(running, position, returned):
                shaped = returned.reshape(n_proj, n_scene, owner_width)
                return lax.dynamic_update_index_in_dim(running, shaped, slot_base + position, 0)

            picker = (
                None
                if source is None
                else lambda position: lax.dynamic_index_in_dim(
                    source, slot_base + position, 0, keepdims=False
                )
            )
            buffer = run_blocks(jac_set, pixel_set, first_pos, last_pos, picker, keeper, buffer)
        arrived = lax.all_to_all(buffer, "scene", split_axis=2, concat_axis=2, tiled=True)
        arrivals = jnp.moveaxis(arrived, 1, 0).reshape(n_proj, -1)
        partial_sum = (
            jnp.zeros((n_proj, g_dev), jnp.float32).at[:, local_ids.reshape(-1)].add(arrivals)
        )
        return lax.psum(partial_sum, "image")

    def norm_dot(residual, precon_res):
        return lax.psum(jnp.sum(residual * precon_res), "scene")

    residual = -lift(proj_jac, back_project(None))
    solution = jnp.zeros_like(residual)
    precon_res = precond * residual
    direction = precon_res
    rz_now = norm_dot(residual, precon_res)
    for iteration in range(ITERS):
        local_proj = project(proj_jac, direction)
        picked = jnp.moveaxis(jnp.take(local_proj, local_ids, axis=1), 0, 1)
        fetched = lax.all_to_all(picked, "scene", split_axis=2, concat_axis=2, tiled=True).reshape(
            total_slots, -1
        )
        image = lift(proj_jac, back_project(fetched)) + damping * direction
        alpha = rz_now / lax.psum(jnp.sum(direction * image), "scene")
        solution = solution + alpha * direction
        residual = residual - alpha * image
        precon_res = precond * residual
        rz_next = norm_dot(residual, precon_res)
        direction = precon_res + rz_next / rz_now * direction
        rz_now = rz_next
    return (solution, residual)


def solution(mesh):
    return jax.shard_map(
        local,
        mesh=mesh,
        in_specs=(
            P(("scene", "image"), None, None),
            P(("scene", "image"), None),
            P(("scene", "image"), None),
            P(),
            P(None, None, "scene"),
            P(None, "scene"),
            P(None, "scene"),
        ),
        out_specs=(P(None, "scene"), P(None, "scene")),
        check_vma=False,
    )
```

profile of v0, /device:TPU:0, one launch (start us, length us, event | category | flops | bytes accessed | tf_op | source)
XLA Modules:
  0.0 308.2 jit_solution(1758452299170405827)
XLA Ops:
  2.1 7.3 %all-to-all-start = ((s32[8,1,128]{2,1,0:T(1,128)}), s32[8,1,128]{2,1,0:T(1,128)S(1)}, u32[]{:S(2)}, u32[]{:S(2)}) async-start(s32[8,1,128]{2,1,0:T(1,128)} %reshape.172), calls=%async_computation | async-start | bytes 8192 | tf_op jit(solution)/shard_map/all_to_all | solution.py:52
  9.4 6.6 %copy.58 = bf16[8,256,1152]{1,2,0:T(8,128)(2,1)} copy(bf16[8,256,1152]{2,1,0:T(8,128)(2,1)} %param.15) | data formatting | bytes 9437184 | tf_op jit(solution)/shard_map/while | solution.py:34
  16.6 27.6 %while.30 = (s32[]{:T(128)}, f32[8,9,8,16]{3,0,1,2:T(8,128)S(1)}, s32[]{:T(128)}, bf16[8,256]{1,0:T(8,128)(2,1)}, bf16[8,256,1152]{1,2,0:T(8,128)(2,1)}, /*index=5*/s32[]{:T(128)}, s32[]{:T(128)}, s32[]{:T(128)}) while((s32[]{:T(128)}, f32[8,9,8,16]{3,0,1,2:T(8,128)S(1)}, s32[]{:T(128)}, bf16[8,256]{1,0:T(8,128)(2,1)}, ...), condition=%wide.region_1.2_spmd, body=%wide.region_0.1_spmd.sunk | while | flops 589829 | bytes 1793675 | solution.py:34
  18.3 1.5 fusion.52
  21.7 1.5 fusion.52
  25.1 1.5 fusion.52
  28.5 1.5 fusion.52
  31.8 1.5 fusion.52
  35.2 1.5 fusion.52
  38.6 1.5 fusion.52
  42.0 1.5 fusion.52
  45.0 6.0 %all-to-all-start.1 = ((f32[8,1,1152]{2,1,0:T(1,128)}), f32[8,1,1152]{2,1,0:T(1,128)S(1)}, u32[]{:S(2)}, u32[]{:S(2)}) async-start(f32[8,1,1152]{2,1,0:T(1,128)} %reshape.174), calls=%async_computation.1 | async-start | bytes 73728 | tf_op jit(solution)/shard_map/all_to_all | solution.py:78
  52.5 5.2 %all-to-all-done.1 = f32[8,1,1152]{2,1,0:T(1,128)S(1)} async-done(((f32[8,1,1152]{2,1,0:T(1,128)}), f32[8,1,1152]{2,1,0:T(1,128)S(1)}, u32[]{:S(2)}, u32[]{:S(2)}) %all-to-all-start.1) | async-done | bytes 36896 | tf_op jit(solution)/shard_map/all_to_all | solution.py:78
  59.7 6.2 %scatter_custom_fusion = f32[9,1024]{0,1:T(8,128)S(1)} fusion(s32[1024]{0:T(1024)S(1)} %bitcast.208, f32[1024,9]{1,0:T(8,128)S(1)} %copy.61, f32[]{:T(128)} %constant.63.clone.1), kind=kCustom, calls=%fused_computation.54 | custom fusion | flops 9216 | bytes 36868 | tf_op jit(solution)/shard_map/scatter-add | solution.py:81
  65.9 16.0 %psum.49 = f32[9,1024]{0,1:T(8,128)S(1)} all-reduce(f32[9,1024]{0,1:T(8,128)S(1)} %scatter_custom_fusion), channel_id=1, replica_groups=mesh['scene'=8,'image'=4] {'image'}, use_global_device_ids=true, to_apply=%region_3.4 | all-reduce | flops 9216 | bytes 73728 | tf_op jit(solution)/shard_map/psum | solution.py:83
  82.9 3.2 %gather_fusion = bf16[1024,9]{1,0:T(8,128)(2,1)S(1)} fusion(bf16[9,1024]{0,1:T(8,128)(2,1)S(1)} %bitcast.187, s32[1024]{0:T(1024)S(1)} %broadcast_clamp_fusion), kind=kCustom, calls=%fused_computation.clone | custom fusion | bytes 40960 | tf_op jit(solution)/shard_map/jit(_take)/gather | solution.py:95
  87.4 3.3 %all-to-all-start.2 = ((bf16[8,2,576]{2,1,0:T(2,128)(2,1)}), bf16[8,2,576]{2,1,0:T(2,128)(2,1)S(1)}, u32[]{:S(2)}, u32[]{:S(2)}) async-start(bf16[8,2,576]{2,1,0:T(2,128)(2,1)} %reshape.176), calls=%async_computation.2 | async-start | bytes 40960 | tf_op jit(solution)/shard_map/all_to_all | solution.py:96
  90.7 6.5 %all-to-all-done.2 = bf16[8,2,576]{2,1,0:T(2,128)(2,1)S(1)} async-done(((bf16[8,2,576]{2,1,0:T(2,128)(2,1)}), bf16[8,2,576]{2,1,0:T(2,128)(2,1)S(1)}, u32[]{:S(2)}, u32[]{:S(2)}) %all-to-all-start.2) | async-done | bytes 18464 | tf_op jit(solution)/shard_map/all_to_all | solution.py:96
  97.6 32.4 %while.31 = (s32[]{:T(128)}, f32[8,9,8,16]{3,0,1,2:T(8,128)S(1)}, s32[]{:T(128)}, bf16[8,256,1152]{1,2,0:T(8,128)(2,1)}, bf16[8,1152]{1,0:T(8,128)(2,1)S(1)}, /*index=5*/s32[]{:T(128)}, s32[]{:T(128)}, s32[]{:T(128)}) while((s32[]{:T(128)}, f32[8,9,8,16]{3,0,1,2:T(8,128)S(1)}, s32[]{:T(128)}, bf16[8,256,1152]{1,2,0:T(8,128)(2,1)}, ...), condition=%wide.region_7.9_spmd, body=%wide.region_6.8_spmd.sunk | while | flops 1179909 | bytes 2392199 | solution.py:34
  130.2 9.1 %all_to_all.30 = f32[8,1,1152]{2,1,0:T(1,128)S(1)} all-to-all(f32[8,1,1152]{2,1,0:T(1,128)S(1)} %reshape.178), channel_id=1, replica_groups=mesh['scene'=8,'image'=4] {'scene'}, dimensions={0} | all-to-all | bytes 73728 | tf_op jit(solution)/shard_map/all_to_all | solution.py:78
  140.7 6.2 %scatter_custom_fusion.1 = f32[9,1024]{0,1:T(8,128)S(1)} fusion(s32[1024]{0:T(1024)S(1)} %bitcast.209, f32[1024,9]{1,0:T(8,128)S(1)} %copy.68, f32[]{:T(128)} %constant.63.clone.1), kind=kCustom, calls=%fused_computation.52 | custom fusion | flops 9216 | bytes 36868 | tf_op jit(solution)/shard_map/scatter-add | solution.py:81
  146.8 16.0 %psum.51 = f32[9,1024]{0,1:T(8,128)S(1)} all-reduce(f32[9,1024]{0,1:T(8,128)S(1)} %scatter_custom_fusion.1), channel_id=1, replica_groups=mesh['scene'=8,'image'=4] {'image'}, use_global_device_ids=true, to_apply=%region_9.11 | all-reduce | flops 9216 | bytes 73728 | tf_op jit(solution)/shard_map/psum | solution.py:83
  164.0 18.4 %all-reduce = (f32[]{:T(128)}, f32[]{:T(128)}) all-reduce(f32[]{:T(128)} %get-tuple-element.151, f32[]{:T(128)} %get-tuple-element.150), channel_id=1, replica_groups=mesh['scene'=8,'image'=4] {'scene'}, use_global_device_ids=true, to_apply=%region_5.6 | all-reduce | flops 2 | bytes 16 | tf_op jit(solution)/shard_map/psum | solution.py:86
  185.2 19.3 %psum.53 = f32[]{:T(128)} all-reduce(f32[]{:T(128)} %get-tuple-element.184), channel_id=1, replica_groups=mesh['scene'=8,'image'=4] {'scene'}, use_global_device_ids=true, to_apply=%region_13.15 | all-reduce | flops 1 | bytes 8 | tf_op jit(solution)/shard_map/psum | solution.py:86
  206.4 3.2 %gather_fusion.1 = bf16[1024,9]{1,0:T(8,128)(2,1)S(1)} fusion(bf16[9,1024]{0,1:T(8,128)(2,1)S(1)} %bitcast.186, s32[1024]{0:T(1024)S(1)} %broadcast_clamp_fusion), kind=kCustom, calls=%fused_computation.1.clone | custom fusion | bytes 40960 | tf_op jit(solution)/shard_map/jit(_take)/gather | solution.py:95
  210.9 3.3 %all-to-all-start.4 = ((bf16[8,2,576]{2,1,0:T(2,128)(2,1)}), bf16[8,2,576]{2,1,0:T(2,128)(2,1)S(1)}, u32[]{:S(2)}, u32[]{:S(2)}) async-start(bf16[8,2,576]{2,1,0:T(2,128)(2,1)} %reshape.180), calls=%async_computation.4 | async-start | bytes 40960 | tf_op jit(solution)/shard_map/all_to_all | solution.py:96
  214.3 6.5 %all-to-all-done.4 = bf16[8,2,576]{2,1,0:T(2,128)(2,1)S(1)} async-done(((bf16[8,2,576]{2,1,0:T(2,128)(2,1)}), bf16[8,2,576]{2,1,0:T(2,128)(2,1)S(1)}, u32[]{:S(2)}, u32[]{:S(2)}) %all-to-all-start.4) | async-done | bytes 18464 | tf_op jit(solution)/shard_map/all_to_all | solution.py:96
  221.2 32.4 %while.32 = (s32[]{:T(128)}, f32[8,9,8,16]{3,0,1,2:T(8,128)S(1)}, s32[]{:T(128)}, bf16[8,256,1152]{1,2,0:T(8,128)(2,1)}, bf16[8,1152]{1,0:T(8,128)(2,1)S(1)}, /*index=5*/s32[]{:T(128)}, s32[]{:T(128)}, s32[]{:T(128)}) while((s32[]{:T(128)}, f32[8,9,8,16]{3,0,1,2:T(8,128)S(1)}, s32[]{:T(128)}, bf16[8,256,1152]{1,2,0:T(8,128)(2,1)}, ...), condition=%wide.region_15.17_spmd, body=%wide.region_14.16_spmd.sunk | while | flops 1179909 | bytes 2392199 | solution.py:34
  253.7 9.1 %all_to_all.31 = f32[8,1,1152]{2,1,0:T(1,128)S(1)} all-to-all(f32[8,1,1152]{2,1,0:T(1,128)S(1)} %reshape.182), channel_id=1, replica_groups=mesh['scene'=8,'image'=4] {'scene'}, dimensions={0} | all-to-all | bytes 73728 | tf_op jit(solution)/shard_map/all_to_all | solution.py:78
  264.2 6.1 %scatter_custom_fusion.2 = f32[9,1024]{0,1:T(8,128)S(1)} fusion(s32[1024]{0:T(1024)S(1)} %bitcast.210, f32[1024,9]{1,0:T(8,128)S(1)} %copy.75, f32[]{:T(128)} %constant.63.clone.1), kind=kCustom, calls=%fused_computation.50 | custom fusion | flops 9216 | bytes 36868 | tf_op jit(solution)/shard_map/scatter-add | solution.py:81
  270.4 16.0 %psum.54 = f32[9,1024]{0,1:T(8,128)S(1)} all-reduce(f32[9,1024]{0,1:T(8,128)S(1)} %scatter_custom_fusion.2), channel_id=1, replica_groups=mesh['scene'=8,'image'=4] {'image'}, use_global_device_ids=true, to_apply=%region_17.19 | all-reduce | flops 9216 | bytes 73728 | tf_op jit(solution)/shard_map/psum | solution.py:83
  287.5 18.4 %psum.55 = f32[]{:T(128)} all-reduce(f32[]{:T(128)} %multiply_reduce_fusion), channel_id=1, replica_groups=mesh['scene'=8,'image'=4] {'scene'}, use_global_device_ids=true, to_apply=%region_19.21 | all-reduce | flops 1 | bytes 8 | tf_op jit(solution)/shard_map/psum | solution.py:100
  (215 shorter events, 83.3 us)
Async XLA Ops:
  2.1 43.0 %all-to-all-start = ((s32[8,1,128]{2,1,0:T(1,128)}), s32[8,1,128]{2,1,0:T(1,128)S(1)}, u32[]{:S(2)}, u32[]{:S(2)}) async-start(s32[8,1,128]{2,1,0:T(1,128)} %reshape.172), calls=%async_computation | async-start | bytes 8192 | tf_op jit(solution)/shard_map/all_to_all | solution.py:52
  9.4 6.7 %copy-start.4 = (s32[32]{0:T(128)S(1)}, s32[32]{0:T(128)}, u32[]{:S(2)}) copy-start(s32[32]{0:T(128)} %param.18) | copy-start | bytes 388
  45.0 12.7 %all-to-all-start.1 = ((f32[8,1,1152]{2,1,0:T(1,128)}), f32[8,1,1152]{2,1,0:T(1,128)S(1)}, u32[]{:S(2)}, u32[]{:S(2)}) async-start(f32[8,1,1152]{2,1,0:T(1,128)} %reshape.174), calls=%async_computation.1 | async-start | bytes 73728 | tf_op jit(solution)/shard_map/all_to_all | solution.py:78
  52.5 29.5 %copy-start = (bf16[9,59,1024]{2,1,0:T(8,128)(2,1)S(1)}, bf16[9,59,1024]{2,1,0:T(8,128)(2,1)}, u32[]{:S(2)}) copy-start(bf16[9,59,1024]{2,1,0:T(8,128)(2,1)} %param.19) | copy-start | bytes 3262468
  59.3 23.1 %copy-start.2 = (f32[59,1024]{1,0:T(8,128)S(1)}, f32[59,1024]{1,0:T(8,128)}, u32[]{:S(2)}) copy-start(f32[59,1024]{1,0:T(8,128)} %param.21) | copy-start | bytes 724996
  87.4 9.9 %all-to-all-start.2 = ((bf16[8,2,576]{2,1,0:T(2,128)(2,1)}), bf16[8,2,576]{2,1,0:T(2,128)(2,1)S(1)}, u32[]{:S(2)}, u32[]{:S(2)}) async-start(bf16[8,2,576]{2,1,0:T(2,128)(2,1)} %reshape.176), calls=%async_computation.2 | async-start | bytes 40960 | tf_op jit(solution)/shard_map/all_to_all | solution.py:96
  140.2 23.0 %copy-start.1 = (f32[59,1024]{1,0:T(8,128)S(1)}, f32[59,1024]{1,0:T(8,128)}, u32[]{:S(2)}) copy-start(f32[59,1024]{1,0:T(8,128)} %param.20) | copy-start | bytes 724996
  210.9 9.9 %all-to-all-start.4 = ((bf16[8,2,576]{2,1,0:T(2,128)(2,1)}), bf16[8,2,576]{2,1,0:T(2,128)(2,1)S(1)}, u32[]{:S(2)}, u32[]{:S(2)}) async-start(bf16[8,2,576]{2,1,0:T(2,128)(2,1)} %reshape.180), calls=%async_computation.4 | async-start | bytes 40960 | tf_op jit(solution)/shard_map/all_to_all | solution.py:96
  264.2 43.1 %copy-start.3 = (f32[59,1024]{1,0:T(8,128)S(1)}, f32[59,1024]{1,0:T(8,128)}, u32[]{:S(2)}) copy-start(f32[59,1024]{1,0:T(8,128)} %get-tuple-element.186) | copy-start | bytes 724996
where the time goes:
time: 311 us; the launch traced here: 308 us
  blocking collectives  122 us (39%)
  local copies, waits for them, and re-layouts  55.8 us (18%)
  matrix products  44.3 us (14%)
  other arithmetic  26.6 us (9%)
  starting transfers between devices  20 us (6%)
  waiting for transfers between devices  18.3 us (6%)
  loops' own time  15.7 us (5%)
  between operations  5.17 us (2%)
    psum x3, blocking collectives, back_project(): return lax.psum(partial_sum, 'image')  48.1 us
    psum x2, blocking collectives, norm_dot(): return lax.psum(jnp.sum(residual * precon_res), 'scene')  37.7 us
    dynamic_slice x24, local copies, waits for them, and re-layouts, advance(): jac_block = lax.dynamic_index_in_dim(jac_set, position, 0, keepdims=False)  26.6 us
    dot_general x24, matrix products, advance(): returned = jnp.dot(signal, jac_block, preferred_element_type=jnp.float32)  24.4 us
    dot_general x16, matrix products, advance(): jnp.dot(jac_block, picker(position), preferred_element_type=jnp.float32)  19.8 us
    scatter-add x3, other arithmetic, back_project(): jnp.zeros((n_proj, g_dev), jnp.float32).at[:, local_ids.reshape(-1)]  18.5 us
    psum x1, blocking collectives, local(): alpha = rz_now / lax.psum(jnp.sum(direction * image), 'scene')  18.4 us
    all_to_all x2, blocking collectives, back_project(): lax.all_to_all(buffer, 'scene', split_axis=2, concat_axis=2, tiled=True)  18.2 us
  transfers between devices with their start and end apart: 4, of which 3 were waited for; matrix products, arithmetic and copies ran while one was open for 10% of the time, Pallas kernels for 0%

commit v1 on v0

--- a/solution.py
+++ b/solution.py
@@ -80,7 +80,7 @@
         partial_sum = (
             jnp.zeros((n_proj, g_dev), jnp.float32).at[:, local_ids.reshape(-1)].add(arrivals)
         )
-        return lax.psum(partial_sum, "image")
+        return jnp.sum(lax.all_gather(partial_sum, "image"), axis=0)
 
     def norm_dot(residual, precon_res):
         return lax.psum(jnp.sum(residual * precon_res), "scene")

time: 311 us -> 280 us (0.900)
  blocking collectives: 122 us -> 91.7 us
    psum x3 -> x0, blocking collectives: 48.1 us -> none  [back_project(): return lax.psum(partial_sum, 'image')]
    all_gather x0 -> x3, blocking collectives: none -> 17.3 us  [back_project(): return jnp.sum(lax.all_gather(partial_sum, 'image'), axis=0)]
  transfers between devices with their start and end apart: 4 -> 4, of which waited for: 3 -> 3; matrix products, arithmetic and copies ran while one was open for 10% -> 12% of each run, Pallas kernels for 0% -> 0%
where the time goes in v1:
time: 280 us; the launch traced here: 277 us
  blocking collectives  91.7 us (33%)
  local copies, waits for them, and re-layouts  55.9 us (20%)
  matrix products  44.3 us (16%)
  other arithmetic  26.1 us (9%)
  starting transfers between devices  20 us (7%)
  waiting for transfers between devices  18.3 us (7%)
  loops' own time  15.7 us (6%)
  between operations  5.11 us (2%)
    psum x2, blocking collectives, norm_dot(): return lax.psum(jnp.sum(residual * precon_res), 'scene')  37.8 us
    dynamic_slice x24, local copies, waits for them, and re-layouts, advance(): jac_block = lax.dynamic_index_in_dim(jac_set, position, 0, keepdims=False)  26.6 us
    dot_general x24, matrix products, advance(): returned = jnp.dot(signal, jac_block, preferred_element_type=jnp.float32)  24.4 us
    dot_general x16, matrix products, advance(): jnp.dot(jac_block, picker(position), preferred_element_type=jnp.float32)  19.9 us
    scatter-add x3, other arithmetic, back_project(): jnp.zeros((n_proj, g_dev), jnp.float32).at[:, local_ids.reshape(-1)]  18.5 us
    psum x1, blocking collectives, local(): alpha = rz_now / lax.psum(jnp.sum(direction * image), 'scene')  18.4 us
    all_to_all x2, blocking collectives, back_project(): lax.all_to_all(buffer, 'scene', split_axis=2, concat_axis=2, tiled=True)  18.2 us
    all_gather x3, blocking collectives, back_project(): return jnp.sum(lax.all_gather(partial_sum, 'image'), axis=0)  17.3 us
  transfers between devices with their start and end apart: 4, of which 3 were waited for; matrix products, arithmetic and copies ran while one was open for 12% of the time, Pallas kernels for 0%

profile of v1, /device:TPU:0, one launch (start us, length us, event | category | flops | bytes accessed | tf_op | source)
XLA Modules:
  0.0 277.1 jit_solution(5634760982652337878)
XLA Ops:
  2.1 7.3 %all-to-all-start = ((s32[8,1,128]{2,1,0:T(1,128)}), s32[8,1,128]{2,1,0:T(1,128)S(1)}, u32[]{:S(2)}, u32[]{:S(2)}) async-start(s32[8,1,128]{2,1,0:T(1,128)} %reshape.184), calls=%async_computation | async-start | bytes 8192 | tf_op jit(solution)/shard_map/all_to_all | solution.py:52
  9.4 6.6 %copy.70 = bf16[8,256,1152]{1,2,0:T(8,128)(2,1)} copy(bf16[8,256,1152]{2,1,0:T(8,128)(2,1)} %param.15) | data formatting | bytes 9437184 | tf_op jit(solution)/shard_map/while | solution.py:34
  16.6 27.7 %while.30 = (s32[]{:T(128)}, f32[8,9,8,16]{3,0,1,2:T(8,128)S(1)}, s32[]{:T(128)}, bf16[8,256]{1,0:T(8,128)(2,1)}, bf16[8,256,1152]{1,2,0:T(8,128)(2,1)}, /*index=5*/s32[]{:T(128)}, s32[]{:T(128)}, s32[]{:T(128)}) while((s32[]{:T(128)}, f32[8,9,8,16]{3,0,1,2:T(8,128)S(1)}, s32[]{:T(128)}, bf16[8,256]{1,0:T(8,128)(2,1)}, ...), condition=%wide.region_1.2_spmd, body=%wide.region_0.1_spmd.sunk | while | flops 589829 | bytes 1793675 | solution.py:34
  18.3 1.5 fusion.52
  21.7 1.5 fusion.52
  25.1 1.5 fusion.52
  28.5 1.5 fusion.52
  31.9 1.5 fusion.52
  35.3 1.5 fusion.52
  38.7 1.5 fusion.52
  42.1 1.5 fusion.52
  45.1 6.0 %all-to-all-start.1 = ((f32[8,1,1152]{2,1,0:T(1,128)}), f32[8,1,1152]{2,1,0:T(1,128)S(1)}, u32[]{:S(2)}, u32[]{:S(2)}) async-start(f32[8,1,1152]{2,1,0:T(1,128)} %reshape.186), calls=%async_computation.1 | async-start | bytes 73728 | tf_op jit(solution)/shard_map/all_to_all | solution.py:78
  52.6 5.2 %all-to-all-done.1 = f32[8,1,1152]{2,1,0:T(1,128)S(1)} async-done(((f32[8,1,1152]{2,1,0:T(1,128)}), f32[8,1,1152]{2,1,0:T(1,128)S(1)}, u32[]{:S(2)}, u32[]{:S(2)}) %all-to-all-start.1) | async-done | bytes 36896 | tf_op jit(solution)/shard_map/all_to_all | solution.py:78
  59.7 6.2 %scatter_custom_fusion = f32[9,1024]{0,1:T(8,128)S(1)} fusion(s32[1024]{0:T(1024)S(1)} %bitcast.217, f32[1024,9]{1,0:T(8,128)S(1)} %copy.73, f32[]{:T(128)} %constant.63.clone.1), kind=kCustom, calls=%fused_computation.54 | custom fusion | flops 9216 | bytes 36868 | tf_op jit(solution)/shard_map/scatter-add | solution.py:81
  66.1 5.8 %all-gather.3 = f32[4,9,1024]{2,1,0:T(8,128)S(1)} all-gather(f32[1,9,1024]{2,1,0:T(8,128)S(1)} %copy.74), channel_id=2, replica_groups=mesh['scene'=8,'image'=4] {'image'}, dimensions={0}, use_global_device_ids=true | all-gather | bytes 184320 | tf_op jit(solution)/shard_map/all_gather | solution.py:83
  72.7 3.2 %gather_fusion = bf16[1024,9]{1,0:T(8,128)(2,1)S(1)} fusion(bf16[9,1024]{0,1:T(8,128)(2,1)S(1)} %bitcast.193, s32[1024]{0:T(1024)S(1)} %broadcast_clamp_fusion), kind=kCustom, calls=%fused_computation.clone | custom fusion | bytes 40960 | tf_op jit(solution)/shard_map/jit(_take)/gather | solution.py:95
  77.2 3.3 %all-to-all-start.2 = ((bf16[8,2,576]{2,1,0:T(2,128)(2,1)}), bf16[8,2,576]{2,1,0:T(2,128)(2,1)S(1)}, u32[]{:S(2)}, u32[]{:S(2)}) async-start(bf16[8,2,576]{2,1,0:T(2,128)(2,1)} %reshape.188), calls=%async_computation.2 | async-start | bytes 40960 | tf_op jit(solution)/shard_map/all_to_all | solution.py:96
  80.5 6.5 %all-to-all-done.2 = bf16[8,2,576]{2,1,0:T(2,128)(2,1)S(1)} async-done(((bf16[8,2,576]{2,1,0:T(2,128)(2,1)}), bf16[8,2,576]{2,1,0:T(2,128)(2,1)S(1)}, u32[]{:S(2)}, u32[]{:S(2)}) %all-to-all-start.2) | async-done | bytes 18464 | tf_op jit(solution)/shard_map/all_to_all | solution.py:96
  87.4 32.4 %while.31 = (s32[]{:T(128)}, f32[8,9,8,16]{3,0,1,2:T(8,128)S(1)}, s32[]{:T(128)}, bf16[8,256,1152]{1,2,0:T(8,128)(2,1)}, bf16[8,1152]{1,0:T(8,128)(2,1)S(1)}, /*index=5*/s32[]{:T(128)}, s32[]{:T(128)}, s32[]{:T(128)}) while((s32[]{:T(128)}, f32[8,9,8,16]{3,0,1,2:T(8,128)S(1)}, s32[]{:T(128)}, bf16[8,256,1152]{1,2,0:T(8,128)(2,1)}, ...), condition=%wide.region_7.9_spmd, body=%wide.region_6.8_spmd.sunk | while | flops 1179909 | bytes 2392199 | solution.py:34
  120.0 9.1 %all_to_all.30 = f32[8,1,1152]{2,1,0:T(1,128)S(1)} all-to-all(f32[8,1,1152]{2,1,0:T(1,128)S(1)} %reshape.190), channel_id=1, replica_groups=mesh['scene'=8,'image'=4] {'scene'}, dimensions={0} | all-to-all | bytes 73728 | tf_op jit(solution)/shard_map/all_to_all | solution.py:78
  130.5 6.2 %scatter_custom_fusion.1 = f32[9,1024]{0,1:T(8,128)S(1)} fusion(s32[1024]{0:T(1024)S(1)} %bitcast.218, f32[1024,9]{1,0:T(8,128)S(1)} %copy.82, f32[]{:T(128)} %constant.63.clone.1), kind=kCustom, calls=%fused_computation.52 | custom fusion | flops 9216 | bytes 36868 | tf_op jit(solution)/shard_map/scatter-add | solution.py:81
  136.9 5.8 %all-gather.4 = f32[4,9,1024]{2,1,0:T(8,128)S(1)} all-gather(f32[1,9,1024]{2,1,0:T(8,128)S(1)} %copy.83), channel_id=3, replica_groups=mesh['scene'=8,'image'=4] {'image'}, dimensions={0}, use_global_device_ids=true | all-gather | bytes 184320 | tf_op jit(solution)/shard_map/all_gather | solution.py:83
  143.7 18.5 %all-reduce = (f32[]{:T(128)}, f32[]{:T(128)}) all-reduce(f32[]{:T(128)} %get-tuple-element.151, f32[]{:T(128)} %get-tuple-element.150), channel_id=1, replica_groups=mesh['scene'=8,'image'=4] {'scene'}, use_global_device_ids=true, to_apply=%region_5.6 | all-reduce | flops 2 | bytes 16 | tf_op jit(solution)/shard_map/psum | solution.py:86
  164.3 19.3 %psum.30 = f32[]{:T(128)} all-reduce(f32[]{:T(128)} %get-tuple-element.184), channel_id=1, replica_groups=mesh['scene'=8,'image'=4] {'scene'}, use_global_device_ids=true, to_apply=%region_13.15 | all-reduce | flops 1 | bytes 8 | tf_op jit(solution)/shard_map/psum | solution.py:86
  185.5 3.2 %gather_fusion.1 = bf16[1024,9]{1,0:T(8,128)(2,1)S(1)} fusion(bf16[9,1024]{0,1:T(8,128)(2,1)S(1)} %bitcast.192, s32[1024]{0:T(1024)S(1)} %broadcast_clamp_fusion), kind=kCustom, calls=%fused_computation.1.clone | custom fusion | bytes 40960 | tf_op jit(solution)/shard_map/jit(_take)/gather | solution.py:95
  190.0 3.3 %all-to-all-start.4 = ((bf16[8,2,576]{2,1,0:T(2,128)(2,1)}), bf16[8,2,576]{2,1,0:T(2,128)(2,1)S(1)}, u32[]{:S(2)}, u32[]{:S(2)}) async-start(bf16[8,2,576]{2,1,0:T(2,128)(2,1)} %reshape.192), calls=%async_computation.4 | async-start | bytes 40960 | tf_op jit(solution)/shard_map/all_to_all | solution.py:96
  193.4 6.5 %all-to-all-done.4 = bf16[8,2,576]{2,1,0:T(2,128)(2,1)S(1)} async-done(((bf16[8,2,576]{2,1,0:T(2,128)(2,1)}), bf16[8,2,576]{2,1,0:T(2,128)(2,1)S(1)}, u32[]{:S(2)}, u32[]{:S(2)}) %all-to-all-start.4) | async-done | bytes 18464 | tf_op jit(solution)/shard_map/all_to_all | solution.py:96
  200.3 32.5 %while.32 = (s32[]{:T(128)}, f32[8,9,8,16]{3,0,1,2:T(8,128)S(1)}, s32[]{:T(128)}, bf16[8,256,1152]{1,2,0:T(8,128)(2,1)}, bf16[8,1152]{1,0:T(8,128)(2,1)S(1)}, /*index=5*/s32[]{:T(128)}, s32[]{:T(128)}, s32[]{:T(128)}) while((s32[]{:T(128)}, f32[8,9,8,16]{3,0,1,2:T(8,128)S(1)}, s32[]{:T(128)}, bf16[8,256,1152]{1,2,0:T(8,128)(2,1)}, ...), condition=%wide.region_15.17_spmd, body=%wide.region_14.16_spmd.sunk | while | flops 1179909 | bytes 2392199 | solution.py:34
  232.9 9.1 %all_to_all.31 = f32[8,1,1152]{2,1,0:T(1,128)S(1)} all-to-all(f32[8,1,1152]{2,1,0:T(1,128)S(1)} %reshape.194), channel_id=1, replica_groups=mesh['scene'=8,'image'=4] {'scene'}, dimensions={0} | all-to-all | bytes 73728 | tf_op jit(solution)/shard_map/all_to_all | solution.py:78
  243.3 6.2 %scatter_custom_fusion.2 = f32[9,1024]{0,1:T(8,128)S(1)} fusion(s32[1024]{0:T(1024)S(1)} %bitcast.219, f32[1024,9]{1,0:T(8,128)S(1)} %copy.91, f32[]{:T(128)} %constant.63.clone.1), kind=kCustom, calls=%fused_computation.50 | custom fusion | flops 9216 | bytes 36868 | tf_op jit(solution)/shard_map/scatter-add | solution.py:81
  249.7 5.8 %all-gather.5 = f32[4,9,1024]{2,1,0:T(8,128)S(1)} all-gather(f32[1,9,1024]{2,1,0:T(8,128)S(1)} %copy.92), channel_id=4, replica_groups=mesh['scene'=8,'image'=4] {'image'}, dimensions={0}, use_global_device_ids=true | all-gather | bytes 184320 | tf_op jit(solution)/shard_map/all_gather | solution.py:83
  256.4 18.4 %psum.31 = f32[]{:T(128)} all-reduce(f32[]{:T(128)} %multiply_reduce_fusion), channel_id=1, replica_groups=mesh['scene'=8,'image'=4] {'scene'}, use_global_device_ids=true, to_apply=%region_19.21 | all-reduce | flops 1 | bytes 8 | tf_op jit(solution)/shard_map/psum | solution.py:100
  (216 shorter events, 83.0 us)
Async XLA Ops:
  2.1 43.0 %all-to-all-start = ((s32[8,1,128]{2,1,0:T(1,128)}), s32[8,1,128]{2,1,0:T(1,128)S(1)}, u32[]{:S(2)}, u32[]{:S(2)}) async-start(s32[8,1,128]{2,1,0:T(1,128)} %reshape.184), calls=%async_computation | async-start | bytes 8192 | tf_op jit(solution)/shard_map/all_to_all | solution.py:52
  9.4 6.7 %copy-start.3 = (s32[32]{0:T(128)S(1)}, s32[32]{0:T(128)}, u32[]{:S(2)}) copy-start(s32[32]{0:T(128)} %param.18) | copy-start | bytes 388
  45.1 12.7 %all-to-all-start.1 = ((f32[8,1,1152]{2,1,0:T(1,128)}), f32[8,1,1152]{2,1,0:T(1,128)S(1)}, u32[]{:S(2)}, u32[]{:S(2)}) async-start(f32[8,1,1152]{2,1,0:T(1,128)} %reshape.186), calls=%async_computation.1 | async-start | bytes 73728 | tf_op jit(solution)/shard_map/all_to_all | solution.py:78
  52.3 19.6 %copy-start = (bf16[9,59,1024]{2,1,0:T(8,128)(2,1)S(1)}, bf16[9,59,1024]{2,1,0:T(8,128)(2,1)}, u32[]{:S(2)}) copy-start(bf16[9,59,1024]{2,1,0:T(8,128)(2,1)} %param.19) | copy-start | bytes 3262468
  59.2 12.9 %copy-start.2 = (f32[59,1024]{1,0:T(8,128)S(1)}, f32[59,1024]{1,0:T(8,128)}, u32[]{:S(2)}) copy-start(f32[59,1024]{1,0:T(8,128)} %param.21) | copy-start | bytes 724996
  77.2 9.9 %all-to-all-start.2 = ((bf16[8,2,576]{2,1,0:T(2,128)(2,1)}), bf16[8,2,576]{2,1,0:T(2,128)(2,1)S(1)}, u32[]{:S(2)}, u32[]{:S(2)}) async-start(bf16[8,2,576]{2,1,0:T(2,128)(2,1)} %reshape.188), calls=%async_computation.2 | async-start | bytes 40960 | tf_op jit(solution)/shard_map/all_to_all | solution.py:96
  130.0 12.9 %copy-start.1 = (f32[59,1024]{1,0:T(8,128)S(1)}, f32[59,1024]{1,0:T(8,128)}, u32[]{:S(2)}) copy-start(f32[59,1024]{1,0:T(8,128)} %param.20) | copy-start | bytes 724996
  190.0 9.9 %all-to-all-start.4 = ((bf16[8,2,576]{2,1,0:T(2,128)(2,1)}), bf16[8,2,576]{2,1,0:T(2,128)(2,1)S(1)}, u32[]{:S(2)}, u32[]{:S(2)}) async-start(bf16[8,2,576]{2,1,0:T(2,128)(2,1)} %reshape.192), calls=%async_computation.4 | async-start | bytes 40960 | tf_op jit(solution)/shard_map/all_to_all | solution.py:96
